TPU v7x, 128 devices: a whole 4x4x4 slice. The times are simulated.
128 devices in a mesh: lat: 8 (over z, x_lo), lon: 16 (over y, x_hi, core).
Axes of the slice: x: 4 (x_hi: 2, x_lo: 2; x = x_hi * 2 + x_lo), y: 4, z: 4, core: 2. Of those that a mesh axis runs over, the one named last changes fastest.
Arguments:
- features: bfloat16 [128, 512, 768], P('lat', 'lon'), may hold values from -10 to 10
- grad_output: bfloat16 [128, 512, 768], P('lat', 'lon'), may hold values from -6 to 6
- qkv_weight: bfloat16 [768, 2304], P(('lat', 'lon')), may hold values from -0.5 to 0.5
- out_weight: bfloat16 [768, 768], P(('lat', 'lon')), may hold values from -0.21875 to 0.21875
Outputs:
- grad_features: bfloat16 [128, 512, 768], P('lat', 'lon')
- grad_qkv_weight: float32 [768, 2304], P(('lat', 'lon'))
- grad_out_weight: float32 [768, 768], P(('lat', 'lon'))
All inputs are finite; a program needn't handle non-finite values.
Results may differ from a plain program's by a relative error of at most 0.018.
Values may be sent and summed in bfloat16 or wider, within the bound.
A program may use at most 128 MiB of HBM per device.

v0:
```python
import math
import jax
import jax.numpy as jnp
from jax import lax
from jax.sharding import PartitionSpec as P

HEADS = 12
RADIUS = 6
QROWS = 16
QCOLS = 16
heads_together = 2


def shifted(value, axis, steps):
    count = lax.axis_size(axis)
    pairs = [(source, (source + steps) % count) for source in range(count)]
    return lax.ppermute(value, axis, pairs)


def shifted_2(value, axis, steps):
    count = lax.axis_size(axis)
    leading, last = (max(0, -steps), min(count, count - steps))
    return lax.ppermute(value, axis, [(source, source + steps) for source in range(leading, last)])


def padded(array, sides, width, wrap):
    for axis, dim in sides:
        devices, length = (lax.axis_size(axis), array.shape[dim])
        up = [(i, (i + 1) % devices) for i in range(devices if wrap else devices - 1)]
        down = [(j, i) for i, j in up]
        last = lax.slice_in_dim(array, length - width, length, axis=dim)
        leading = lax.slice_in_dim(array, 0, width, axis=dim)
        before = lax.ppermute(last, axis, up)
        after = lax.ppermute(leading, axis, down)
        array = jnp.concatenate([before, array, after], axis=dim)
    return array


def window_mask(row_first, query_rows, query_cols, key_rows, key_cols, radius, total_rows):
    q_rows = row_first + jnp.arange(query_rows, dtype=jnp.int32)
    k_rows = row_first - radius + jnp.arange(key_rows, dtype=jnp.int32)
    row_start = jnp.clip(q_rows - radius, 0, total_rows - 2 * radius - 1)
    row_valid = (k_rows[None, :] >= row_start[:, None]) & (
        k_rows[None, :] <= row_start[:, None] + 2 * radius
    )
    q_cols = jnp.arange(query_cols, dtype=jnp.int32)
    k_cols = jnp.arange(key_cols, dtype=jnp.int32)
    col_valid = (k_cols[None, :] >= q_cols[:, None]) & (
        k_cols[None, :] <= q_cols[:, None] + 2 * radius
    )
    allowed = row_valid[:, None, :, None] & col_valid[None, :, None, :]
    return allowed.reshape(query_rows * query_cols, key_rows * key_cols)


def tile_terms(queries, keys, values, grad_heads, window, head_count, head_dim):
    q_count = queries.shape[0]
    k_count = keys.shape[0]
    softmax_scale = 1.0 / math.sqrt(head_dim)
    query_h = queries.reshape(q_count, head_count, head_dim)
    key_h = keys.reshape(k_count, head_count, head_dim)
    value_h = values.reshape(k_count, head_count, head_dim)
    grad_h = grad_heads.reshape(q_count, head_count, head_dim)
    scores = (
        jnp.einsum("qhe,khe->hqk", query_h, key_h, preferred_element_type=jnp.float32)
        * softmax_scale
    )
    scores = jnp.where(window[None], scores, -jnp.inf)
    row_max = jnp.max(scores, axis=2, keepdims=True)
    exp_terms = jnp.exp(scores - row_max)
    prob_f32 = exp_terms / jnp.sum(exp_terms, axis=2, keepdims=True)
    prob_b16 = prob_f32.astype(jnp.bfloat16)
    attended = jnp.einsum(
        "hqk,khe->qhe", prob_b16, value_h, preferred_element_type=jnp.float32
    ).astype(jnp.bfloat16)
    row_term = jnp.sum(grad_h.astype(jnp.float32) * attended.astype(jnp.float32), axis=2)
    dprob = jnp.einsum("qhe,khe->hqk", grad_h, value_h, preferred_element_type=jnp.float32)
    dscore = (prob_f32 * (dprob - row_term.T[:, :, None])).astype(jnp.bfloat16)
    grad_query = jnp.einsum("hqk,khe->qhe", dscore, key_h, preferred_element_type=jnp.float32)
    grad_key = jnp.einsum("hqk,qhe->khe", dscore, query_h, preferred_element_type=jnp.float32)
    grad_value = jnp.einsum("hqk,qhe->khe", prob_b16, grad_h, preferred_element_type=jnp.float32)
    model_part = head_count * head_dim
    return (
        attended.reshape(q_count, model_part),
        grad_query.reshape(q_count, model_part),
        grad_key.reshape(k_count, model_part),
        grad_value.reshape(k_count, model_part),
    )


def turn_lon(strip_part, offset):
    return shifted(strip_part.astype(jnp.bfloat16), "lon", offset).astype(strip_part.dtype)


def turn_lat(strip_part, offset):
    return shifted_2(strip_part.astype(jnp.bfloat16), "lat", offset).astype(strip_part.dtype)


def shards(features, grad_output, qkv_weight, out_weight):
    lat_rows, lon_cols, model_width = features.shape
    radius = RADIUS
    head_dim = model_width // HEADS
    qkv_full, out_full = (
        lax.all_gather(qkv_weight, ("lat", "lon"), axis=0, tiled=True),
        lax.all_gather(out_weight, ("lat", "lon"), axis=0, tiled=True),
    )
    x_rows = features.reshape(-1, model_width)
    grad_rows = grad_output.reshape(-1, model_width)
    projected = jnp.dot(x_rows, qkv_full, preferred_element_type=jnp.float32).astype(jnp.bfloat16)
    projected = projected.reshape(lat_rows, lon_cols, 3 * model_width)
    grad_attn = lax.dot_general(
        grad_rows, out_full, (((1,), (1,)), ((), ())), preferred_element_type=jnp.float32
    )
    grad_attn = grad_attn.astype(jnp.bfloat16).reshape(lat_rows, lon_cols, model_width)
    queries = projected[..., :model_width]
    key_value = projected[..., model_width:]
    lon_wide = padded(key_value, (("lon", 1),), radius, True)
    extended = padded(lon_wide, (("lat", 0),), radius, False)
    total_rows = lat_rows * lax.axis_size("lat")
    lat_first = lax.axis_index("lat") * lat_rows
    key_rows = QROWS + 2 * radius
    key_cols = QCOLS + 2 * radius
    wide_cols = lon_cols + 2 * radius
    grad_kv = jnp.zeros((lat_rows + 2 * radius, wide_cols, 2 * model_width), jnp.float32)
    window = window_mask(lat_first + 0, QROWS, QCOLS, key_rows, key_cols, radius, total_rows)
    out_row = []
    query_row = []
    for col_index in range(lon_cols // QCOLS):
        left_col = col_index * QCOLS
        q_tile = queries[0:QROWS, left_col : left_col + QCOLS].reshape(-1, model_width)
        g_tile = grad_attn[0:QROWS, left_col : left_col + QCOLS].reshape(-1, model_width)
        kv_tile = extended[0:key_rows, left_col : left_col + key_cols].reshape(-1, 2 * model_width)
        out_parts, query_parts, key_parts, value_parts = ([], [], [], [])
        for first_head in range(0, HEADS, heads_together):
            col_low = first_head * head_dim
            col_high = col_low + heads_together * head_dim
            attended, grad_query, grad_key, grad_value = tile_terms(
                q_tile[:, col_low:col_high],
                kv_tile[:, col_low:col_high],
                kv_tile[:, model_width + col_low : model_width + col_high],
                g_tile[:, col_low:col_high],
                window,
                heads_together,
                head_dim,
            )
            out_parts.append(attended)
            query_parts.append(grad_query)
            key_parts.append(grad_key)
            value_parts.append(grad_value)
        out_row.append(jnp.concatenate(out_parts, axis=1).reshape(QROWS, QCOLS, model_width))
        query_row.append(jnp.concatenate(query_parts, axis=1).reshape(QROWS, QCOLS, model_width))
        key_part = jnp.concatenate(key_parts + value_parts, axis=1).reshape(
            key_rows, key_cols, 2 * model_width
        )
        grad_kv = grad_kv.at[0:key_rows, left_col : left_col + key_cols].add(key_part)
    out_blocks = jnp.concatenate(out_row, axis=1)
    query_blocks = jnp.concatenate(query_row, axis=1)
    from_right = turn_lon(grad_kv[:, :radius], -1)
    from_left = turn_lon(grad_kv[:, wide_cols - radius :], 1)
    middle = grad_kv[:, radius : radius + lon_cols]
    middle = middle.at[:, :radius].add(from_left)
    middle = middle.at[:, lon_cols - radius :].add(from_right)
    from_below = turn_lat(middle[:radius], -1)
    from_above = turn_lat(middle[lat_rows + radius :], 1)
    interior = middle[radius : radius + lat_rows]
    interior = interior.at[:radius].add(from_above)
    interior = interior.at[lat_rows - radius :].add(from_below)
    softmax_scale = 1.0 / math.sqrt(head_dim)
    query_all = query_blocks.reshape(-1, model_width)
    grad_query = (query_all * softmax_scale).astype(jnp.bfloat16)
    grad_key = (
        (interior[..., :model_width] * softmax_scale).astype(jnp.bfloat16).reshape(-1, model_width)
    )
    grad_value = interior[..., model_width:].astype(jnp.bfloat16).reshape(-1, model_width)
    grad_proj = jnp.concatenate([grad_query, grad_key, grad_value], axis=1)
    attended_rows = out_blocks.reshape(-1, model_width)
    grad_features = lax.dot_general(
        grad_proj, qkv_full, (((1,), (1,)), ((), ())), preferred_element_type=jnp.float32
    )
    grad_features = grad_features.astype(jnp.bfloat16).reshape(lat_rows, lon_cols, model_width)
    first_term = lax.dot_general(
        x_rows, grad_proj, (((0,), (0,)), ((), ())), preferred_element_type=jnp.float32
    )
    second_term = lax.dot_general(
        attended_rows, grad_rows, (((0,), (0,)), ((), ())), preferred_element_type=jnp.float32
    )
    my_grads = lax.psum_scatter(
        jnp.concatenate([first_term, second_term], axis=1),
        ("lat", "lon"),
        scatter_dimension=0,
        tiled=True,
    )
    return (grad_features, my_grads[:, : 3 * model_width], my_grads[:, 3 * model_width :])


def solution(mesh):
    placed = (
        P("lat", "lon", None),
        P("lat", "lon", None),
        P(("lat", "lon"), None),
        P(("lat", "lon"), None),
    )
    return jax.shard_map(
        shards,
        mesh=mesh,
        in_specs=placed,
        out_specs=(P("lat", "lon", None), P(("lat", "lon"), None), P(("lat", "lon"), None)),
        check_vma=False,
    )
```

profile of v0, /device:TPU:1, one launch (start us, length us, event | category | flops | bytes accessed | tf_op | source)
XLA Modules:
  0.0 1026.2 jit_solution(18377570423413452368)
XLA Ops:
  9.5 3.4 and.58
  13.8 194.4 %all-gather.7.cloned.1.call-done = bf16[128,6,768]{2,1,0:T(8,128)(2,1)} async-done(((bf16[1,6,768]{2,1,0:T(8,128)(2,1)}), bf16[128,6,768]{2,1,0:T(8,128)(2,1)}) %all-gather.7.cloned.1.call-update) | async-done | bytes 1179664 | tf_op jit(solution)/shard_map/all_gather | solution.py:104
  212.3 194.4 %all-gather.5.cloned.1.call-done = bf16[128,6,2304]{2,1,0:T(8,128)(2,1)} async-done(((bf16[1,6,2304]{2,1,0:T(8,128)(2,1)}), bf16[128,6,2304]{2,1,0:T(8,128)(2,1)}) %all-gather.5.cloned.1.call-update) | async-done | bytes 3538960 | tf_op jit(solution)/shard_map/all_gather | solution.py:103
  406.7 6.6 reshape.732
  413.3 4.0 convolution_convert_fusion
  417.4 2.9 collective-permute-start
  420.6 4.8 collective-permute-done
  425.4 6.1 collective-permute-done.1
  433.4 3.5 collective-permute-start.2
  475.8 3.0 pad_maximum_fusion.1
  480.9 4.8 reshape.701
  485.7 3.2 fusion.97
  492.5 2.9 exponential_reduce_fusion.4
  504.6 2.9 exponential_reduce_fusion.5
  516.9 2.9 exponential_reduce_fusion.3
  529.1 2.9 exponential_reduce_fusion.2
  544.2 3.1 fusion.98
  573.4 3.3 exponential_reduce_fusion.8
  584.9 3.4 exponential_reduce_fusion.7
  596.5 3.4 exponential_reduce_fusion.6
  727.5 2.8 constant_dynamic-update-slice_fusion.48
  730.3 2.5 slice.521
  775.0 6.3 slice.492
  788.1 7.2 scatter-add.24
  797.0 6.4 scatter-add.25
  803.4 2.9 convert.15
  807.6 4.3 collective-permute-start.6
  819.6 13.0 %collective-permute-done.7 = bf16[6,32,1536]{2,1,0:T(8,128)(2,1)S(1)} collective-permute-done((bf16[6,32,1536]{2,1,0:T(8,128)(2,1)}, bf16[6,32,1536]{2,1,0:T(8,128)(2,1)S(1)}, u32[]{:S(2)}, u32[]{:S(2)}) %collective-permute-start.7) | collective-permute-done | bytes 589856 | tf_op jit(solution)/shard_map/ppermute | solution.py:23
  834.1 4.9 convolution_bitcast_fusion
  839.0 7.2 pad_maximum_fusion
  846.3 5.2 convolution_convert_fusion.2
  851.4 162.9 %all-reduce.4.cloned.1.call-done = f32[768,3072]{0,1:T(8,128)} async-done(((f32[768,3072]{0,1:T(8,128)}), f32[768,3072]{0,1:T(8,128)}) %all-reduce.4.cloned.1.call-update) | async-done | bytes 9437200
  (659 shorter events, 328.7 us)
Async XLA Ops:
  7.2 406.1 %copy-start = (bf16[16,32,768]{2,1,0:T(8,128)(2,1)S(1)}, bf16[16,32,768]{2,1,0:T(8,128)(2,1)}, u32[]{:S(2)}) copy-start(bf16[16,32,768]{2,1,0:T(8,128)(2,1)} %param.16) | copy-start | bytes 2359300
  7.2 201.1 %all-gather.7.cloned.1.call-start = ((), (), s32[]{:S(2)}) async-start(), calls=%async_computation.1 | async-start | bytes 1585152 | tf_op jit(solution)/shard_map/all_gather | solution.py:104
  7.9 398.8 %all-gather.5.cloned.1.call-start = ((), (), s32[]{:S(2)}) async-start(), calls=%async_computation | async-start | bytes 4755456 | tf_op jit(solution)/shard_map/all_gather | solution.py:103
  8.7 1005.7 %all-reduce.4.cloned.1.call-start = ((), (), s32[]{:S(2)}) async-start(), calls=%async_computation.2 | async-start | bytes 18874368
  12.8 197.7 %copy-start.87 = (bf16[16,32,768]{2,1,0:T(8,128)(2,1)S(1)}, bf16[16,32,768]{2,1,0:T(8,128)(2,1)}, u32[]{:S(2)}) copy-start(bf16[16,32,768]{2,1,0:T(8,128)(2,1)} %param.17) | copy-start | bytes 2359300
  417.4 8.0 collective-permute-start
  420.3 11.2 %collective-permute-start.1 = (bf16[16,6,1536]{2,1,0:T(8,128)(2,1)S(1)}, bf16[16,6,1536]{2,1,0:T(8,128)(2,1)S(1)}, u32[]{:S(2)}, u32[]{:S(2)}) collective-permute-start(bf16[16,6,1536]{2,1,0:T(8,128)(2,1)S(1)} %get-tuple-element.119), channel_id=1, source_target_pairs={{1,0},{2,1},{3,2},{4,3},{5,4},{6,5},{7,6},{8,7},{9,8},{10,9},{11,1... | collective-permute-start | bytes 884744 | tf_op jit(solution)/shard_map/ppermute | solution.py:34
  433.4 40.9 %collective-permute-start.2 = (bf16[6,44,1536]{2,1,0:T(8,128)(2,1)}, bf16[6,44,1536]{2,1,0:T(8,128)(2,1)}, u32[]{:S(2)}, u32[]{:S(2)}) collective-permute-start(bf16[6,44,1536]{2,1,0:T(8,128)(2,1)} %get-tuple-element.116), channel_id=1, source_target_pairs={{0,16},{16,32},{32,48},{48,64},{64,80},{80,96},{96,112},{1,17},{17... | collective-permute-start | bytes 2433032 | tf_op jit(solution)/shard_map/ppermute | solution.py:33
  436.9 38.9 %collective-permute-start.3 = (bf16[6,44,1536]{2,1,0:T(8,128)(2,1)}, bf16[6,44,1536]{2,1,0:T(8,128)(2,1)}, u32[]{:S(2)}, u32[]{:S(2)}) collective-permute-start(bf16[6,44,1536]{2,1,0:T(8,128)(2,1)} %get-tuple-element.117), channel_id=1, source_target_pairs={{16,0},{32,16},{48,32},{64,48},{80,64},{96,80},{112,96},{17,1},{33... | collective-permute-start | bytes 2433032 | tf_op jit(solution)/shard_map/ppermute | solution.py:34
  635.5 20.0 %copy-start.14 = (bf16[2,256,784]{1,2,0:T(8,128)(2,1)}, bf16[2,256,784]{1,2,0:T(8,128)(2,1)S(1)}, u32[]{:S(2)}) copy-start(bf16[2,256,784]{1,2,0:T(8,128)(2,1)S(1)} %multiply_convert_fusion) | copy-start | bytes 2408452
  701.6 19.9 %slice-start = ((s8[5505024]{0:T(1024)(128)(4,1)}), s8[1310720]{0:T(1024)(128)(4,1)S(1)}, s32[]{:S(2)}) async-start(s8[5505024]{0:T(1024)(128)(4,1)} %bitcast.341), calls=%async_computation.3 | async-start | bytes 2621440
  711.5 7.3 copy-start.22
  713.6 7.9 slice-start.1
  733.8 51.9 %collective-permute-start.4 = (bf16[28,6,1536]{2,0,1:T(8,128)(2,1)}, bf16[28,6,1536]{2,0,1:T(8,128)(2,1)}, u32[]{:S(2)}, u32[]{:S(2)}) collective-permute-start(bf16[28,6,1536]{2,0,1:T(8,128)(2,1)} %copy.253), channel_id=1, source_target_pairs={{0,1},{1,2},{2,3},{3,4},{4,5},{5,6},{6,7},{7,8},{8,9},{9,10},{10,1... | collective-permute-start | bytes 1548296 | tf_op jit(solution)/shard_map/ppermute | solution.py:17
  734.9 18.0 %copy-start.124 = (bf16[256,2,64]{0,2,1:T(8,128)(2,1)S(1)}, bf16[256,2,64]{0,2,1:T(8,128)(2,1)}, u32[]{:S(2)}) copy-start(bf16[256,2,64]{0,2,1:T(8,128)(2,1)} %get-tuple-element.177) | copy-start | bytes 196612
  734.9 60.3 %collective-permute-start.5 = (bf16[28,6,1536]{2,0,1:T(8,128)(2,1)}, bf16[28,6,1536]{2,0,1:T(8,128)(2,1)S(1)}, u32[]{:S(2)}, u32[]{:S(2)}) collective-permute-start(bf16[28,6,1536]{2,0,1:T(8,128)(2,1)} %copy.255), channel_id=1, source_target_pairs={{0,15},{1,0},{2,1},{3,2},{4,3},{5,4},{6,5},{7,6},{8,7},{9,8},{10,9... | collective-permute-start | bytes 1548296 | tf_op jit(solution)/shard_map/ppermute | solution.py:17
  738.3 26.9 %copy-start.56 = (f32[16,16,768]{2,1,0:T(8,128)S(1)}, f32[16,16,768]{2,1,0:T(8,128)}, u32[]{:S(2)}) copy-start(f32[16,16,768]{2,1,0:T(8,128)} %constant_dynamic-update-slice_fusion.5) | copy-start | bytes 2359300
  738.3 26.9 %copy-start.121 = (f32[16,16,128]{2,1,0:T(8,128)S(1)}, f32[16,16,128]{2,1,0:T(8,128)}, u32[]{:S(2)}) copy-start(f32[16,16,128]{2,1,0:T(8,128)} %concatenate.153) | copy-start | bytes 393220
  755.4 16.9 %copy-start.129 = (bf16[16,16,128]{2,1,0:T(8,128)(2,1)S(1)}, bf16[16,16,128]{2,1,0:T(8,128)(2,1)}, u32[]{:S(2)}) copy-start(bf16[16,16,128]{2,1,0:T(8,128)(2,1)} %concatenate.195) | copy-start | bytes 196612
  765.2 7.0 copy-start.130
  765.3 7.1 copy-start.131
  765.3 7.1 copy-start.132
  765.3 7.1 copy-start.133
  765.3 7.1 copy-start.134
  765.3 7.8 copy-start.135
  765.3 8.4 copy-start.136
  765.3 9.1 copy-start.137
  775.0 8.8 copy-start.61
  806.4 6.4 copy-start.119
  806.4 6.8 copy-start.59
  807.6 10.9 %collective-permute-start.6 = (bf16[6,32,1536]{2,1,0:T(8,128)(2,1)}, bf16[6,32,1536]{2,1,0:T(8,128)(2,1)}, u32[]{:S(2)}, u32[]{:S(2)}) collective-permute-start(bf16[6,32,1536]{2,1,0:T(8,128)(2,1)} %get-tuple-element.89), channel_id=1, source_target_pairs={{0,16},{16,32},{32,48},{48,64},{64,80},{80,96},{96,112},{1,17},{17... | collective-permute-start | bytes 1769480 | tf_op jit(solution)/shard_map/ppermute | solution.py:23
  815.2 17.4 %collective-permute-start.7 = (bf16[6,32,1536]{2,1,0:T(8,128)(2,1)}, bf16[6,32,1536]{2,1,0:T(8,128)(2,1)S(1)}, u32[]{:S(2)}, u32[]{:S(2)}) collective-permute-start(bf16[6,32,1536]{2,1,0:T(8,128)(2,1)} %get-tuple-element.88), channel_id=1, source_target_pairs={{16,0},{32,16},{48,32},{64,48},{80,64},{96,80},{112,96},{17,1},{33... | collective-permute-start | bytes 1769480 | tf_op jit(solution)/shard_map/ppermute | solution.py:23
  (146 other events, 392.9 us)
Sparse Core Ops, SparseCore 0:
  9.7 198.4 all-gather.6
  210.0 196.7 all-gather.4
  846.4 167.9 all-reduce.3
where the time goes:
time: 1040 us; the launch traced here: 1030 us
  waiting for transfers between devices  580 us (56%)
  local copies, waits for them, and re-layouts  268 us (26%)
  matrix products  103 us (10%)
  other arithmetic  44.1 us (4%)
  between operations  15.9 us (2%)
  starting transfers between devices  14.7 us (1%)
    all_gather x1, waiting for transfers between devices, shards(): lax.all_gather(qkv_weight, ('lat', 'lon'), axis=0, tiled=True)  194 us
    all_gather x1, waiting for transfers between devices, shards(): lax.all_gather(out_weight, ('lat', 'lon'), axis=0, tiled=True)  194 us
    unnamed x4, waiting for transfers between devices  164 us
    unnamed x428, local copies, waits for them, and re-layouts  101 us
    concatenate x26, local copies, waits for them, and re-layouts, shards(): jnp.concatenate(key_parts + value_parts, axis=1)  36.7 us
    sub x12, matrix products, tile_terms(): exp_terms = jnp.exp(scores - row_max)  29.7 us
  transfers between devices with their start and end apart: 11, of which 8 were waited for; matrix products, arithmetic and copies ran while one was open for 11% of the time, Pallas kernels for 0%

commit v1 on v0

--- a/solution.py
+++ b/solution.py
@@ -100,7 +100,12 @@
     radius = RADIUS
     head_dim = model_width // HEADS
     qkv_full, out_full = (
-        lax.all_gather(qkv_weight, ("lat", "lon"), axis=0, tiled=True),
+        jnp.concatenate(
+            lax.all_to_all(
+                jnp.stack([qkv_weight] * lax.axis_size(("lat", "lon"))), ("lat", "lon"), 0, 0
+            ),
+            axis=0,
+        ),
         lax.all_gather(out_weight, ("lat", "lon"), axis=0, tiled=True),
     )
     x_rows = features.reshape(-1, model_width)

time: 1040 us -> 881 us (0.85)
  waiting for transfers between devices: 580 us -> 406 us
  starting transfers between devices: 14.7 us -> 28.3 us
    all_gather x1 -> x0, waiting for transfers between devices: 194 us -> none  [shards(): lax.all_gather(qkv_weight, ('lat', 'lon'), axis=0, tiled=True)]
    all_gather x1, waiting for transfers between devices: 194 us -> 216 us  [shards(): lax.all_gather(out_weight, ('lat', 'lon'), axis=0, tiled=True)]
    all_to_all x0 -> x1, starting transfers between devices: none -> 11.9 us  [shards(): lax.all_to_all(jnp.stack([qkv_weight] * lax.axis_size(('lat', 'lon'))), (...]
    unnamed x428 -> x427, local copies, waits for them, and re-layouts: 101 us -> 94.4 us
    unnamed x4 -> x3, waiting for transfers between devices: 164 us -> 163 us
  transfers between devices with their start and end apart: 11 -> 11, of which waited for: 8 -> 6; matrix products, arithmetic and copies ran while one was open for 11% -> 13% of each run, Pallas kernels for 0% -> 0%
where the time goes in v1:
time: 881 us; the launch traced here: 869 us
  waiting for transfers between devices  406 us (46%)
  local copies, waits for them, and re-layouts  272 us (31%)
  matrix products  103 us (12%)
  other arithmetic  44.1 us (5%)
  starting transfers between devices  28.3 us (3%)
  between operations  16.2 us (2%)
    all_gather x1, waiting for transfers between devices, shards(): lax.all_gather(out_weight, ('lat', 'lon'), axis=0, tiled=True)  216 us
    unnamed x3, waiting for transfers between devices  163 us
    unnamed x427, local copies, waits for them, and re-layouts  94.4 us
    concatenate x26, local copies, waits for them, and re-layouts, shards(): jnp.concatenate(key_parts + value_parts, axis=1)  36.6 us
    sub x12, matrix products, tile_terms(): exp_terms = jnp.exp(scores - row_max)  29.7 us
    convert_element_type x12, other arithmetic, tile_terms(): prob_b16 = prob_f32.astype(jnp.bfloat16)  19.6 us
    transpose x12, local copies, waits for them, and re-layouts, tile_terms(): jnp.einsum('hqk,qhe->khe', prob_b16, grad_h, preferred_element_type=jnp.f...  19 us
  transfers between devices with their start and end apart: 11, of which 6 were waited for; matrix products, arithmetic and copies ran while one was open for 13% of the time, Pallas kernels for 0%

profile of v1, /device:TPU:1, one launch (start us, length us, event | category | flops | bytes accessed | tf_op | source)
XLA Modules:
  0.0 869.3 jit_solution(5284112072988623556)
XLA Ops:
  7.2 3.4 stack.2
  10.5 11.9 %all-to-all-start = ((bf16[128,6,2304]{2,1,0:T(8,128)(2,1)}), bf16[128,6,2304]{2,1,0:T(8,128)(2,1)}, u32[]{:S(2)}, u32[]{:S(2)}) async-start(bf16[128,6,2304]{2,1,0:T(8,128)(2,1)} %stack.2), calls=%async_computation | async-start | bytes 9437184 | tf_op jit(solution)/shard_map/all_to_all | solution.py:104
  24.0 3.4 and.58
  28.3 215.9 %all-gather.3.cloned.1.call-done = bf16[128,6,768]{2,1,0:T(8,128)(2,1)} async-done(((bf16[1,6,768]{2,1,0:T(8,128)(2,1)}), bf16[128,6,768]{2,1,0:T(8,128)(2,1)}) %all-gather.3.cloned.1.call-update) | async-done | bytes 1179664 | tf_op jit(solution)/shard_map/all_gather | solution.py:109
  248.3 6.6 reshape.676
  254.9 4.0 convolution_convert_fusion
  259.0 2.9 collective-permute-start
  262.1 4.8 collective-permute-done
  266.9 7.5 collective-permute-done.1
  316.0 3.0 pad_maximum_fusion.1
  321.1 4.8 reshape.707
  325.9 3.2 fusion.97
  332.6 2.9 exponential_reduce_fusion.4
  344.8 2.9 exponential_reduce_fusion.5
  357.0 2.9 exponential_reduce_fusion.3
  369.2 2.9 exponential_reduce_fusion.2
  384.4 3.2 fusion.98
  413.5 3.3 exponential_reduce_fusion.8
  425.1 3.3 exponential_reduce_fusion.7
  436.6 3.4 exponential_reduce_fusion.6
  567.6 2.8 constant_dynamic-update-slice_fusion.48
  570.4 2.5 slice.521
  616.9 6.3 slice.492
  629.9 7.2 scatter-add.24
  638.8 6.4 scatter-add.25
  645.2 2.9 convert.15
  649.4 5.4 collective-permute-start.6
  662.6 13.8 %collective-permute-done.7 = bf16[6,32,1536]{2,1,0:T(8,128)(2,1)S(1)} collective-permute-done((bf16[6,32,1536]{2,1,0:T(8,128)(2,1)}, bf16[6,32,1536]{2,1,0:T(8,128)(2,1)S(1)}, u32[]{:S(2)}, u32[]{:S(2)}) %collective-permute-start.7) | collective-permute-done | bytes 589856 | tf_op jit(solution)/shard_map/ppermute | solution.py:23
  677.8 4.9 convolution_bitcast_fusion
  682.7 7.2 pad_maximum_fusion
  690.0 5.2 convolution_convert_fusion.2
  695.2 162.0 %all-reduce.4.cloned.1.call-done = f32[768,3072]{0,1:T(8,128)} async-done(((f32[768,3072]{0,1:T(8,128)}), f32[768,3072]{0,1:T(8,128)}) %all-reduce.4.cloned.1.call-update) | async-done | bytes 9437200
  (659 shorter events, 330.4 us)
Async XLA Ops:
  7.2 247.7 %copy-start = (bf16[16,32,768]{2,1,0:T(8,128)(2,1)S(1)}, bf16[16,32,768]{2,1,0:T(8,128)(2,1)}, u32[]{:S(2)}) copy-start(bf16[16,32,768]{2,1,0:T(8,128)(2,1)} %param.16) | copy-start | bytes 2359300
  10.5 237.7 %all-to-all-start = ((bf16[128,6,2304]{2,1,0:T(8,128)(2,1)}), bf16[128,6,2304]{2,1,0:T(8,128)(2,1)}, u32[]{:S(2)}, u32[]{:S(2)}) async-start(bf16[128,6,2304]{2,1,0:T(8,128)(2,1)} %stack.2), calls=%async_computation | async-start | bytes 9437184 | tf_op jit(solution)/shard_map/all_to_all | solution.py:104
  22.4 221.8 %all-gather.3.cloned.1.call-start = ((), (), s32[]{:S(2)}) async-start(), calls=%async_computation.1 | async-start | bytes 1585152 | tf_op jit(solution)/shard_map/all_gather | solution.py:109
  23.2 833.9 %all-reduce.4.cloned.1.call-start = ((), (), s32[]{:S(2)}) async-start(), calls=%async_computation.2 | async-start | bytes 18874368
  27.4 219.2 %copy-start.87 = (bf16[16,32,768]{2,1,0:T(8,128)(2,1)S(1)}, bf16[16,32,768]{2,1,0:T(8,128)(2,1)}, u32[]{:S(2)}) copy-start(bf16[16,32,768]{2,1,0:T(8,128)(2,1)} %param.17) | copy-start | bytes 2359300
  259.0 7.9 collective-permute-start
  261.9 12.5 %collective-permute-start.1 = (bf16[16,6,1536]{2,1,0:T(8,128)(2,1)S(1)}, bf16[16,6,1536]{2,1,0:T(8,128)(2,1)S(1)}, u32[]{:S(2)}, u32[]{:S(2)}) collective-permute-start(bf16[16,6,1536]{2,1,0:T(8,128)(2,1)S(1)} %get-tuple-element.119), channel_id=1, source_target_pairs={{1,0},{2,1},{3,2},{4,3},{5,4},{6,5},{7,6},{8,7},{9,8},{10,9},{11,1... | collective-permute-start | bytes 884744 | tf_op jit(solution)/shard_map/ppermute | solution.py:34
  276.3 39.7 %collective-permute-start.2 = (bf16[6,44,1536]{2,1,0:T(8,128)(2,1)}, bf16[6,44,1536]{2,1,0:T(8,128)(2,1)}, u32[]{:S(2)}, u32[]{:S(2)}) collective-permute-start(bf16[6,44,1536]{2,1,0:T(8,128)(2,1)} %get-tuple-element.116), channel_id=1, source_target_pairs={{0,16},{16,32},{32,48},{48,64},{64,80},{80,96},{96,112},{1,17},{17... | collective-permute-start | bytes 2433032 | tf_op jit(solution)/shard_map/ppermute | solution.py:33
  278.6 37.3 %collective-permute-start.3 = (bf16[6,44,1536]{2,1,0:T(8,128)(2,1)}, bf16[6,44,1536]{2,1,0:T(8,128)(2,1)}, u32[]{:S(2)}, u32[]{:S(2)}) collective-permute-start(bf16[6,44,1536]{2,1,0:T(8,128)(2,1)} %get-tuple-element.117), channel_id=1, source_target_pairs={{16,0},{32,16},{48,32},{64,48},{80,64},{96,80},{112,96},{17,1},{33... | collective-permute-start | bytes 2433032 | tf_op jit(solution)/shard_map/ppermute | solution.py:34
  475.7 20.0 %copy-start.14 = (bf16[2,256,784]{1,2,0:T(8,128)(2,1)}, bf16[2,256,784]{1,2,0:T(8,128)(2,1)S(1)}, u32[]{:S(2)}) copy-start(bf16[2,256,784]{1,2,0:T(8,128)(2,1)S(1)} %multiply_convert_fusion) | copy-start | bytes 2408452
  541.7 19.9 %slice-start = ((s8[5505024]{0:T(1024)(128)(4,1)}), s8[1310720]{0:T(1024)(128)(4,1)S(1)}, s32[]{:S(2)}) async-start(s8[5505024]{0:T(1024)(128)(4,1)} %bitcast.340), calls=%async_computation.3 | async-start | bytes 2621440
  551.6 7.4 copy-start.22
  553.7 7.9 slice-start.1
  573.9 53.6 %collective-permute-start.4 = (bf16[28,6,1536]{2,0,1:T(8,128)(2,1)}, bf16[28,6,1536]{2,0,1:T(8,128)(2,1)}, u32[]{:S(2)}, u32[]{:S(2)}) collective-permute-start(bf16[28,6,1536]{2,0,1:T(8,128)(2,1)} %copy.253), channel_id=1, source_target_pairs={{0,1},{1,2},{2,3},{3,4},{4,5},{5,6},{6,7},{7,8},{8,9},{9,10},{10,1... | collective-permute-start | bytes 1548296 | tf_op jit(solution)/shard_map/ppermute | solution.py:17
  576.4 18.4 %copy-start.124 = (bf16[256,2,64]{0,2,1:T(8,128)(2,1)S(1)}, bf16[256,2,64]{0,2,1:T(8,128)(2,1)}, u32[]{:S(2)}) copy-start(bf16[256,2,64]{0,2,1:T(8,128)(2,1)} %get-tuple-element.177) | copy-start | bytes 196612
  576.4 60.7 %collective-permute-start.5 = (bf16[28,6,1536]{2,0,1:T(8,128)(2,1)}, bf16[28,6,1536]{2,0,1:T(8,128)(2,1)S(1)}, u32[]{:S(2)}, u32[]{:S(2)}) collective-permute-start(bf16[28,6,1536]{2,0,1:T(8,128)(2,1)} %copy.255), channel_id=1, source_target_pairs={{0,15},{1,0},{2,1},{3,2},{4,3},{5,4},{6,5},{7,6},{8,7},{9,8},{10,9... | collective-permute-start | bytes 1548296 | tf_op jit(solution)/shard_map/ppermute | solution.py:17
  580.1 27.0 %copy-start.56 = (f32[16,16,768]{2,1,0:T(8,128)S(1)}, f32[16,16,768]{2,1,0:T(8,128)}, u32[]{:S(2)}) copy-start(f32[16,16,768]{2,1,0:T(8,128)} %constant_dynamic-update-slice_fusion.5) | copy-start | bytes 2359300
  580.1 27.0 %copy-start.121 = (f32[16,16,128]{2,1,0:T(8,128)S(1)}, f32[16,16,128]{2,1,0:T(8,128)}, u32[]{:S(2)}) copy-start(f32[16,16,128]{2,1,0:T(8,128)} %concatenate.153) | copy-start | bytes 393220
  597.2 16.9 %copy-start.129 = (bf16[16,16,128]{2,1,0:T(8,128)(2,1)S(1)}, bf16[16,16,128]{2,1,0:T(8,128)(2,1)}, u32[]{:S(2)}) copy-start(bf16[16,16,128]{2,1,0:T(8,128)(2,1)} %concatenate.195) | copy-start | bytes 196612
  607.1 7.1 copy-start.131
  607.1 7.1 copy-start.132
  607.1 7.1 copy-start.133
  607.1 7.1 copy-start.134
  607.1 7.8 copy-start.135
  607.1 8.5 copy-start.136
  607.1 9.1 %copy-start.137 = (bf16[16,16,128]{2,1,0:T(8,128)(2,1)S(1)}, bf16[16,16,128]{2,1,0:T(8,128)(2,1)}, u32[]{:S(2)}) copy-start(bf16[16,16,128]{2,1,0:T(8,128)(2,1)} %concatenate.205) | copy-start | bytes 196612
  616.9 8.8 %copy-start.61 = (bf16[784,128]{0,1:T(8,128)(2,1)S(1)}, bf16[784,128]{0,1:T(8,128)(2,1)}, u32[]{:S(2)}) copy-start(bf16[784,128]{0,1:T(8,128)(2,1)} %copy-done.60) | copy-start | bytes 602116
  648.2 7.3 copy-start.120
  648.2 7.6 copy-start.119
  648.2 8.0 copy-start.59
  649.4 12.0 %collective-permute-start.6 = (bf16[6,32,1536]{2,1,0:T(8,128)(2,1)}, bf16[6,32,1536]{2,1,0:T(8,128)(2,1)}, u32[]{:S(2)}, u32[]{:S(2)}) collective-permute-start(bf16[6,32,1536]{2,1,0:T(8,128)(2,1)} %get-tuple-element.89), channel_id=1, source_target_pairs={{0,16},{16,32},{32,48},{48,64},{64,80},{80,96},{96,112},{1,17},{17... | collective-permute-start | bytes 1769480 | tf_op jit(solution)/shard_map/ppermute | solution.py:23
  658.2 18.2 %collective-permute-start.7 = (bf16[6,32,1536]{2,1,0:T(8,128)(2,1)}, bf16[6,32,1536]{2,1,0:T(8,128)(2,1)S(1)}, u32[]{:S(2)}, u32[]{:S(2)}) collective-permute-start(bf16[6,32,1536]{2,1,0:T(8,128)(2,1)} %get-tuple-element.88), channel_id=1, source_target_pairs={{16,0},{32,16},{48,32},{64,48},{80,64},{96,80},{112,96},{17,1},{33... | collective-permute-start | bytes 1769480 | tf_op jit(solution)/shard_map/ppermute | solution.py:23
  (146 other events, 402.5 us)
Sparse Core Ops, SparseCore 0:
  25.0 219.2 all-gather.2
  690.1 166.9 all-reduce.3
